TPU v7x, 128 devices: a whole 4x4x4 slice. The times are simulated.
128 devices in a mesh: prow: 16 (over x, z_hi, core), pcol: 8 (over z_lo, y).
Axes of the slice: x: 4, y: 4, z: 4 (z_hi: 2, z_lo: 2; z = z_hi * 2 + z_lo), core: 2. Of those that a mesh axis runs over, the one named last changes fastest.
Arguments:
- inverse: bfloat16 [4, 8192, 8, 4096], P(None, 'prow', None, 'pcol'), may hold values from -6 to 6
- panel: bfloat16 [2, 4, 8192, 256], P(None, None, 'prow'), may hold values from -0.0625 to 0.0625
- structure: int32 [2, 16], replicated, may hold values from 0 to 63, as said below
- diag_inverse: float32 [2, 256, 256], replicated, may hold values from -6 to 6
Outputs:
- off_diag: bfloat16 [2, 4, 8192, 256], P(None, None, ('prow', 'pcol'))
- diag_block: float32 [2, 256, 256], replicated
Inputs may be any that keep to these rules, and one draw needn't show every extreme that they name: `structure`: each row lists 16 distinct block indices in increasing order, exactly one of them congruent to p modulo 16 for every p, and always includes the last ancestor block 63.
All inputs are finite; a program needn't handle non-finite values.
Results may differ from a plain program's by a relative error of at most 0.0022.
Values may be sent and summed in bfloat16 or wider, within the bound.
No kernel may reach another device: no remote copies, remote signals or barrier semaphores. Data moves between devices by JAX's collectives and lax.ppermute only.
A program may use at most 128 MiB of HBM per device.

v0:
```python
import jax
import jax.numpy as jnp
from jax import lax
from jax.sharding import PartitionSpec as P


def cut_along(array, dim, count):
    before, after = (array.shape[:dim], array.shape[dim + 1 :])
    return jnp.moveaxis(array.reshape(*before, count, -1, *after), dim, 0)


def sum_at_owner(array, axis, dim):
    tiles = cut_along(array, dim, lax.axis_size(axis))
    arrived = lax.all_to_all(tiles, axis, split_axis=0, concat_axis=0, tiled=True)
    return arrived.sum(axis=0)


def on_device(inverse, panel, structure, diag_inverse):
    prow_count = lax.axis_size("prow")
    pcol_count = lax.axis_size("pcol")
    prow_index = lax.axis_index("prow")
    pcol_index = lax.axis_index("pcol")
    rows_local, block_size, cols_local, _ = inverse.shape
    panel_width = panel.shape[3]
    total_blocks = rows_local * prow_count
    piece_rows = block_size // pcol_count
    owner_ratio = prow_count // pcol_count
    repeat_count = cols_local // owner_ratio
    positions = jnp.arange(total_blocks, dtype=jnp.int32)
    local_rows = jnp.arange(rows_local, dtype=jnp.int32)
    pieces = []
    products = []
    for supernode in range(structure.shape[0]):
        chosen = structure[supernode]
        selected = jnp.any(chosen[:, None] == positions[None, :], axis=0)
        own_rows = lax.dynamic_index_in_dim(
            selected.reshape(rows_local, prow_count), prow_index, 1, keepdims=False
        )
        own_cols = lax.dynamic_index_in_dim(
            selected.reshape(cols_local, pcol_count), pcol_index, 1, keepdims=False
        )
        local_panel = panel[supernode]
        row_pick = jnp.sum(jnp.where(own_rows, local_rows, 0))
        single = lax.dynamic_index_in_dim(local_panel, row_pick, 0, keepdims=False)
        gathered = lax.all_gather(single, "prow", axis=0, tiled=True)
        gathered = gathered.reshape(owner_ratio, pcol_count, block_size, panel_width)
        owner_blocks = lax.dynamic_index_in_dim(gathered, pcol_index, 1, keepdims=False)
        tiled = jnp.broadcast_to(
            owner_blocks[None], (repeat_count, owner_ratio, block_size, panel_width)
        )
        tiled = tiled.reshape(cols_local, block_size, panel_width)
        column_panel = tiled * own_cols.astype(jnp.bfloat16)[:, None, None]
        ranking = jnp.where(own_cols, 0, cols_local) + jnp.arange(cols_local, dtype=jnp.int32)
        column_order = jnp.argsort(ranking)
        live_count = jnp.sum(own_cols.astype(jnp.int32))

        def add_column(position_index, running):
            column = column_order[position_index]
            block_column = lax.dynamic_index_in_dim(inverse, column, 2, keepdims=False)
            factor = lax.dynamic_index_in_dim(column_panel, column, 0, keepdims=False)
            return running + jnp.einsum(
                "rab,bw->raw", block_column, factor, preferred_element_type=jnp.float32
            )

        starting = jnp.zeros((rows_local, block_size, panel_width), jnp.float32)
        partial_value = lax.fori_loop(0, live_count, add_column, starting)
        partial_value = -partial_value * own_rows.astype(jnp.float32)[:, None, None]
        summed = sum_at_owner(partial_value, "pcol", 1)
        rounded = summed.astype(jnp.bfloat16)
        pieces.append(rounded)
        factor_rows = lax.dynamic_slice_in_dim(local_panel, pcol_index * piece_rows, piece_rows, 1)
        products.append(
            jnp.einsum("raw,rav->wv", factor_rows, rounded, preferred_element_type=jnp.float32)
        )
    diagonal_terms = lax.psum(jnp.stack(products), ("prow", "pcol"))
    return (jnp.stack(pieces), diag_inverse - diagonal_terms)


def solution(mesh):
    placed = (P(None, "prow", None, "pcol"), P(None, None, "prow", None), P(), P())
    return jax.shard_map(
        on_device,
        mesh=mesh,
        in_specs=placed,
        out_specs=(P(None, None, ("prow", "pcol"), None), P()),
        check_vma=False,
    )
```

profile of v0, /device:TPU:1, one launch (start us, length us, event | category | flops | bytes accessed | tf_op | source)
XLA Modules:
  0.0 347.8 jit_solution(9517647593599522379)
XLA Ops:
  7.2 0.8 slice_bitcast_fusion.1
  8.0 0.1 fusion.24
  8.3 0.2 fusion.28
  8.5 0.2 fusion.29
  8.7 0.6 select_reduce_fusion.2
  10.6 1.7 fusion.30
  13.0 0.7 constant_dynamic-slice_fusion.3
  15.7 0.7 constant_dynamic-slice_fusion
  16.7 16.7 %copy.16 = bf16[4,512,8,512]{3,1,0,2:T(8,128)(2,1)} copy(bf16[4,512,8,512]{3,2,1,0:T(8,128)(2,1)} %param.8) | data formatting | bytes 33554432 | tf_op jit(solution)/shard_map/while | solution.py:66
  33.3 0.2 convert_reduce_fusion.3
  33.5 0.8 select_reduce_fusion.1
  34.3 1.0 sort.31
  35.3 0.8 select_reduce_fusion
  36.1 37.5 %all-gather.5.cloned.1.call-done = bf16[1,1,8192,256]{3,2,1,0:T(8,128)(2,1)} async-done(((bf16[1,1,512,256]{3,2,1,0:T(8,128)(2,1)}), bf16[1,1,8192,256]{3,2,1,0:T(8,128)(2,1)}) %all-gather.5.cloned.1.call-update) | async-done | bytes 4194320 | tf_op jit(solution)/shard_map/all_gather | solution.py:45
  73.6 1.1 dynamic-slice_bitcast_fusion.1
  74.7 1.6 bitcast_multiply_fusion.1
  76.2 0.2 broadcast.9.clone.1
  76.4 11.7 %while.20 = (s32[]{:T(128)}, f32[4,512,256]{2,1,0:T(8,128)S(1)}, s32[]{:T(128)}, s32[8]{0:T(128)S(1)}, bf16[4,512,8,512]{3,1,0,2:T(8,128)(2,1)}, /*index=5*/bf16...) while((s32[]{:T(128)}, f32[4,512,256]{2,1,0:T(8,128)S(1)}, s32[]{:T(128)}, s32[8]{0:T(128)S(1)}, ...), condition=%wide.region_5.6_spmd, body=%wide.region_4.5_spmd.sunk | while | flops 537395200 | bytes 6554797 | solution.py:66
  77.1 0.6 dynamic_slice.130
  79.6 2.3 fusion.41
  82.5 0.6 dynamic_slice.130
  85.1 2.4 fusion.41
  88.1 0.3 negate_multiply_fusion.1
  88.4 1.5 copy.17
  89.9 4.3 %all-to-all-start = ((f32[8,4,64,256]{3,2,1,0:T(8,128)}), f32[8,4,64,256]{3,2,1,0:T(8,128)}, u32[]{:S(2)}, u32[]{:S(2)}) async-start(f32[8,4,64,256]{3,2,1,0:T(8,128)} %copy.17), calls=%async_computation | async-start | bytes 4194304 | tf_op jit(solution)/shard_map/all_to_all | solution.py:14
  94.2 0.2 convert_reduce_fusion.2
  94.4 1.0 sort.32
  95.5 45.2 %all-gather.7.cloned.1.call-done = bf16[1,1,8192,256]{3,2,1,0:T(8,128)(2,1)} async-done(((bf16[1,1,512,256]{3,2,1,0:T(8,128)(2,1)}), bf16[1,1,8192,256]{3,2,1,0:T(8,128)(2,1)}) %all-gather.7.cloned.1.call-update) | async-done | bytes 4194320 | tf_op jit(solution)/shard_map/all_gather | solution.py:45
  140.7 1.1 dynamic-slice_bitcast_fusion
  141.7 1.6 bitcast_multiply_fusion
  143.3 0.2 broadcast.9.clone
  143.5 11.8 %while.21 = (s32[]{:T(128)}, f32[4,512,256]{2,1,0:T(8,128)S(1)}, s32[]{:T(128)}, s32[8]{0:T(128)S(1)}, bf16[4,512,8,512]{3,1,0,2:T(8,128)(2,1)}, /*index=5*/bf16...) while((s32[]{:T(128)}, f32[4,512,256]{2,1,0:T(8,128)S(1)}, s32[]{:T(128)}, s32[8]{0:T(128)S(1)}, ...), condition=%wide.region_12.13_spmd, body=%wide.region_11.12_spmd.sunk | while | flops 537395200 | bytes 6554797 | solution.py:66
  144.2 0.6 dynamic_slice.133
  146.7 2.3 fusion.44
  149.8 0.6 dynamic_slice.133
  152.3 2.3 fusion.44
  155.3 0.3 negate_multiply_fusion
  155.6 1.5 copy.19
  157.1 4.3 %all-to-all-start.1 = ((f32[8,4,64,256]{3,2,1,0:T(8,128)}), f32[8,4,64,256]{3,2,1,0:T(8,128)S(1)}, u32[]{:S(2)}, u32[]{:S(2)}) async-start(f32[8,4,64,256]{3,2,1,0:T(8,128)} %copy.19), calls=%async_computation.1 | async-start | bytes 4194304 | tf_op jit(solution)/shard_map/all_to_all | solution.py:14
  161.4 1.7 reduce_sum.56
  163.1 1.8 convolution_bitcast_fusion.1
  165.0 23.5 %all-to-all-done.1 = f32[8,4,64,256]{3,2,1,0:T(8,128)S(1)} async-done(((f32[8,4,64,256]{3,2,1,0:T(8,128)}), f32[8,4,64,256]{3,2,1,0:T(8,128)S(1)}, u32[]{:S(2)}, u32[]{:S(2)}) %all-to-all-start.1) | async-done | bytes 2097184 | tf_op jit(solution)/shard_map/all_to_all | solution.py:14
  188.5 0.1 reduce_sum.59
  188.6 0.2 convolution_bitcast_fusion
  188.8 1.8 pad_maximum_fusion
  190.6 0.7 pad_maximum_fusion.1
  191.4 148.0 %all-reduce.2.cloned.1.call-done = f32[2,256,256]{2,1,0:T(8,128)} async-done(((f32[2,256,256]{2,1,0:T(8,128)}), f32[2,256,256]{2,1,0:T(8,128)}) %all-reduce.2.cloned.1.call-update) | async-done | bytes 524304 | tf_op jit(solution)/shard_map/psum | solution.py:75
  339.4 1.9 sub.3
  (22 shorter events, 0.6 us)
Async XLA Ops:
  7.2 66.4 %all-gather.5.cloned.1.call-start = ((), (), s32[]{:S(2)}) async-start(), calls=%async_computation.3 | async-start | bytes 4456448 | tf_op jit(solution)/shard_map/all_gather | solution.py:45
  12.3 21.0 %copy-start = (bf16[1,4,512,256]{3,2,1,0:T(8,128)(2,1)}, bf16[1,4,512,256]{3,2,1,0:T(8,128)(2,1)S(1)}, u32[]{:S(2)}) copy-start(bf16[1,4,512,256]{3,2,1,0:T(8,128)(2,1)S(1)} %get-tuple-element.162) | copy-start | bytes 3145732
  13.7 126.9 %all-gather.7.cloned.1.call-start = ((), (), s32[]{:S(2)}) async-start(), calls=%async_computation.4 | async-start | bytes 4456448 | tf_op jit(solution)/shard_map/all_gather | solution.py:45
  89.9 67.2 %all-to-all-start = ((f32[8,4,64,256]{3,2,1,0:T(8,128)}), f32[8,4,64,256]{3,2,1,0:T(8,128)}, u32[]{:S(2)}, u32[]{:S(2)}) async-start(f32[8,4,64,256]{3,2,1,0:T(8,128)} %copy.17), calls=%async_computation | async-start | bytes 4194304 | tf_op jit(solution)/shard_map/all_to_all | solution.py:14
  157.1 31.4 %all-to-all-start.1 = ((f32[8,4,64,256]{3,2,1,0:T(8,128)}), f32[8,4,64,256]{3,2,1,0:T(8,128)S(1)}, u32[]{:S(2)}, u32[]{:S(2)}) async-start(f32[8,4,64,256]{3,2,1,0:T(8,128)} %copy.19), calls=%async_computation.1 | async-start | bytes 4194304 | tf_op jit(solution)/shard_map/all_to_all | solution.py:14
  161.4 178.0 %all-reduce.2.cloned.1.call-start = ((), (), s32[]{:S(2)}) async-start(), calls=%async_computation.2 | async-start | bytes 1048576 | tf_op jit(solution)/shard_map/psum | solution.py:75
  188.6 150.8 %copy-start.1 = (f32[2,256,256]{2,1,0:T(8,128)S(1)}, f32[2,256,256]{2,1,0:T(8,128)}, u32[]{:S(2)}) copy-start(f32[2,256,256]{2,1,0:T(8,128)} %param.11) | copy-start | bytes 1572868
Sparse Core Ops, SparseCore 0:
  13.9 59.6 all-gather.4
  76.6 64.0 all-gather.6
  190.8 148.5 all-reduce.1
where the time goes:
time: 349 us; the launch traced here: 348 us
  waiting for transfers between devices  254 us (73%)
  local copies, waits for them, and re-layouts  29.1 us (8%)
  between operations  17.8 us (5%)
  other arithmetic  14.8 us (4%)
  loops' own time  11.8 us (3%)
  matrix products  11.4 us (3%)
  starting transfers between devices  8.73 us (3%)
    psum x1, waiting for transfers between devices, on_device(): diagonal_terms = lax.psum(jnp.stack(products), ('prow', 'pcol'))  148 us
    all_gather x2, waiting for transfers between devices, on_device(): gathered = lax.all_gather(single, 'prow', axis=0, tiled=True)  82.7 us
    all_to_all x2, waiting for transfers between devices, sum_at_owner(): lax.all_to_all(tiles, axis, split_axis=0, concat_axis=0, tiled=True)  23.5 us
    while x1, local copies, waits for them, and re-layouts, on_device(): partial_value = lax.fori_loop(0, live_count, add_column, starting)  16.7 us
    another operation x2, loops' own time, on_device(): partial_value = lax.fori_loop(0, live_count, add_column, starting)  11.8 us
    dot_general x4, matrix products, add_column(): jnp.einsum('rab,bw->raw', block_column, factor, preferred_element_type=jn...  9.32 us
    all_to_all x2, starting transfers between devices, sum_at_owner(): lax.all_to_all(tiles, axis, split_axis=0, concat_axis=0, tiled=True)  8.61 us
  transfers between devices with their start and end apart: 5, of which 4 were waited for; matrix products, arithmetic and copies ran while one was open for 13% of the time, Pallas kernels for 0%

commit v1 on v0

--- a/solution.py
+++ b/solution.py
@@ -42,7 +42,9 @@
         local_panel = panel[supernode]
         row_pick = jnp.sum(jnp.where(own_rows, local_rows, 0))
         single = lax.dynamic_index_in_dim(local_panel, row_pick, 0, keepdims=False)
-        gathered = lax.all_gather(single, "prow", axis=0, tiled=True)
+        gathered = jnp.concatenate(
+            lax.all_to_all(jnp.stack([single] * lax.axis_size("prow")), "prow", 0, 0), axis=0
+        )
         gathered = gathered.reshape(owner_ratio, pcol_count, block_size, panel_width)
         owner_blocks = lax.dynamic_index_in_dim(gathered, pcol_index, 1, keepdims=False)
         tiled = jnp.broadcast_to(

time: 349 us -> 374 us (1.072)
  starting transfers between devices: 8.73 us -> 35 us
    all_gather x2 -> x0, waiting for transfers between devices: 82.7 us -> none  [on_device(): gathered = lax.all_gather(single, 'prow', axis=0, tiled=True)]
    all_to_all x0 -> x2, waiting for transfers between devices: none -> 68.4 us  [on_device(): lax.all_to_all(jnp.stack([single] * lax.axis_size('prow')), 'prow', 0, 0)]
    all_to_all x0 -> x2, starting transfers between devices: none -> 22.1 us  [on_device(): lax.all_to_all(jnp.stack([single] * lax.axis_size('prow')), 'prow', 0, 0)]
    all_to_all x2, waiting for transfers between devices: 23.5 us -> 33.8 us  [sum_at_owner(): lax.all_to_all(tiles, axis, split_axis=0, concat_axis=0, tiled=True)]
    another operation x2 -> x4, local copies, waits for them, and re-layouts: 0.31 us -> 5.02 us  [the longest x2 4.71 us: on_device(): jnp.stack([single] * lax.axis_size('prow'))]
    all_to_all x2, starting transfers between devices: 8.61 us -> 12.9 us  [sum_at_owner(): lax.all_to_all(tiles, axis, split_axis=0, concat_axis=0, tiled=True)]
  transfers between devices with their start and end apart: 5 -> 5, of which waited for: 4 -> 5; matrix products, arithmetic and copies ran while one was open for 13% -> 12% of each run, Pallas kernels for 0% -> 0%
where the time goes in v1:
time: 374 us; the launch traced here: 373 us
  waiting for transfers between devices  252 us (67%)
  starting transfers between devices  35 us (9%)
  local copies, waits for them, and re-layouts  32.2 us (9%)
  between operations  18.1 us (5%)
  other arithmetic  14.6 us (4%)
  matrix products  11.3 us (3%)
  loops' own time  10.5 us (3%)
    psum x1, waiting for transfers between devices, on_device(): diagonal_terms = lax.psum(jnp.stack(products), ('prow', 'pcol'))  149 us
    all_to_all x2, waiting for transfers between devices, on_device(): lax.all_to_all(jnp.stack([single] * lax.axis_size('prow')), 'prow', 0, 0)  68.4 us
    all_to_all x2, waiting for transfers between devices, sum_at_owner(): lax.all_to_all(tiles, axis, split_axis=0, concat_axis=0, tiled=True)  33.8 us
    all_to_all x2, starting transfers between devices, on_device(): lax.all_to_all(jnp.stack([single] * lax.axis_size('prow')), 'prow', 0, 0)  22.1 us
    while x1, local copies, waits for them, and re-layouts, on_device(): partial_value = lax.fori_loop(0, live_count, add_column, starting)  16.6 us
    all_to_all x2, starting transfers between devices, sum_at_owner(): lax.all_to_all(tiles, axis, split_axis=0, concat_axis=0, tiled=True)  12.9 us
    another operation x2, loops' own time, on_device(): partial_value = lax.fori_loop(0, live_count, add_column, starting)  10.5 us
    dot_general x4, matrix products, add_column(): jnp.einsum('rab,bw->raw', block_column, factor, preferred_element_type=jn...  9.23 us
  transfers between devices with their start and end apart: 5, of which 5 were waited for; matrix products, arithmetic and copies ran while one was open for 12% of the time, Pallas kernels for 0%

profile of v1, /device:TPU:1, one launch (start us, length us, event | category | flops | bytes accessed | tf_op | source)
XLA Modules:
  0.0 373.4 jit_solution(6146794443949422200)
XLA Ops:
  7.2 0.8 slice_bitcast_fusion.1
  8.3 0.2 fusion.28
  8.5 0.2 fusion.29
  8.7 0.6 select_reduce_fusion.2
  10.6 1.7 fusion.30
  13.0 2.3 stack.12
  15.3 9.1 %all-to-all-start = ((bf16[16,512,256]{2,1,0:T(8,128)(2,1)}), bf16[16,512,256]{2,1,0:T(8,128)(2,1)}, u32[]{:S(2)}, u32[]{:S(2)}) async-start(bf16[16,512,256]{2,1,0:T(8,128)(2,1)} %stack.12), calls=%async_computation | async-start | bytes 8388608 | tf_op jit(solution)/shard_map/all_to_all | solution.py:46
  26.4 50.7 %all-to-all-done = bf16[16,512,256]{2,1,0:T(8,128)(2,1)} async-done(((bf16[16,512,256]{2,1,0:T(8,128)(2,1)}), bf16[16,512,256]{2,1,0:T(8,128)(2,1)}, u32[]{:S(2)}, u32[]{:S(2)}) %all-to-all-start) | async-done | bytes 4194336 | tf_op jit(solution)/shard_map/all_to_all | solution.py:46
  77.2 2.4 stack.13
  79.5 13.0 %all-to-all-start.2 = ((bf16[16,512,256]{2,1,0:T(8,128)(2,1)}), bf16[16,512,256]{2,1,0:T(8,128)(2,1)}, u32[]{:S(2)}, u32[]{:S(2)}) async-start(bf16[16,512,256]{2,1,0:T(8,128)(2,1)} %stack.13), calls=%async_computation.2 | async-start | bytes 8388608 | tf_op jit(solution)/shard_map/all_to_all | solution.py:46
  92.7 16.6 %copy.16 = bf16[4,512,8,512]{3,1,0,2:T(8,128)(2,1)} copy(bf16[4,512,8,512]{3,2,1,0:T(8,128)(2,1)} %param.8) | data formatting | bytes 33554432 | tf_op jit(solution)/shard_map/while | solution.py:68
  109.3 0.2 convert_reduce_fusion.3
  109.5 0.7 select_reduce_fusion.1
  110.2 1.0 sort.31
  111.2 0.7 select_reduce_fusion
  111.9 1.1 dynamic-slice_bitcast_fusion.1
  112.9 1.6 bitcast_multiply_fusion.1
  114.6 0.2 broadcast.11.clone.1
  114.7 11.0 %while.20 = (s32[]{:T(128)}, f32[4,512,256]{2,1,0:T(8,128)S(1)}, s32[]{:T(128)}, s32[8]{0:T(128)S(1)}, bf16[4,512,8,512]{3,1,0,2:T(8,128)(2,1)}, /*index=5*/bf16...) while((s32[]{:T(128)}, f32[4,512,256]{2,1,0:T(8,128)S(1)}, s32[]{:T(128)}, s32[8]{0:T(128)S(1)}, ...), condition=%wide.region_5.6_spmd, body=%wide.region_4.5_spmd.sunk | while | flops 537395200 | bytes 6554797 | solution.py:68
  115.4 0.6 dynamic_slice.136
  117.6 2.3 fusion.41
  120.6 0.6 dynamic_slice.136
  122.8 2.3 fusion.41
  125.7 0.3 negate_multiply_fusion.1
  126.0 1.5 copy.17
  127.5 17.7 %all-to-all-done.2 = bf16[16,512,256]{2,1,0:T(8,128)(2,1)} async-done(((bf16[16,512,256]{2,1,0:T(8,128)(2,1)}), bf16[16,512,256]{2,1,0:T(8,128)(2,1)}, u32[]{:S(2)}, u32[]{:S(2)}) %all-to-all-start.2) | async-done | bytes 4194336 | tf_op jit(solution)/shard_map/all_to_all | solution.py:46
  145.2 4.6 %all-to-all-start.1 = ((f32[8,4,64,256]{3,2,1,0:T(8,128)}), f32[8,4,64,256]{3,2,1,0:T(8,128)}, u32[]{:S(2)}, u32[]{:S(2)}) async-start(f32[8,4,64,256]{3,2,1,0:T(8,128)} %copy.17), calls=%async_computation.1 | async-start | bytes 4194304 | tf_op jit(solution)/shard_map/all_to_all | solution.py:14
  149.9 0.2 convert_reduce_fusion.2
  150.1 1.0 sort.32
  151.1 1.1 dynamic-slice_bitcast_fusion
  152.1 1.6 bitcast_multiply_fusion
  153.9 11.0 %while.21 = (s32[]{:T(128)}, f32[4,512,256]{2,1,0:T(8,128)S(1)}, s32[]{:T(128)}, s32[8]{0:T(128)S(1)}, bf16[4,512,8,512]{3,1,0,2:T(8,128)(2,1)}, /*index=5*/bf16...) while((s32[]{:T(128)}, f32[4,512,256]{2,1,0:T(8,128)S(1)}, s32[]{:T(128)}, s32[8]{0:T(128)S(1)}, ...), condition=%wide.region_12.13_spmd, body=%wide.region_11.12_spmd.sunk | while | flops 537395200 | bytes 6554797 | solution.py:68
  154.6 0.6 dynamic_slice.139
  156.8 2.3 fusion.44
  159.7 0.6 dynamic_slice.139
  161.9 2.3 fusion.44
  164.9 0.3 negate_multiply_fusion
  165.2 1.5 copy.19
  166.7 10.4 %all-to-all-done.1 = f32[8,4,64,256]{3,2,1,0:T(8,128)} async-done(((f32[8,4,64,256]{3,2,1,0:T(8,128)}), f32[8,4,64,256]{3,2,1,0:T(8,128)}, u32[]{:S(2)}, u32[]{:S(2)}) %all-to-all-start.1) | async-done | bytes 2097184 | tf_op jit(solution)/shard_map/all_to_all | solution.py:14
  177.1 8.2 %all-to-all-start.3 = ((f32[8,4,64,256]{3,2,1,0:T(8,128)}), f32[8,4,64,256]{3,2,1,0:T(8,128)S(1)}, u32[]{:S(2)}, u32[]{:S(2)}) async-start(f32[8,4,64,256]{3,2,1,0:T(8,128)} %copy.19), calls=%async_computation.3 | async-start | bytes 4194304 | tf_op jit(solution)/shard_map/all_to_all | solution.py:14
  185.4 1.7 reduce_sum.56
  187.1 1.8 convolution_bitcast_fusion.1
  189.0 23.4 %all-to-all-done.3 = f32[8,4,64,256]{3,2,1,0:T(8,128)S(1)} async-done(((f32[8,4,64,256]{3,2,1,0:T(8,128)}), f32[8,4,64,256]{3,2,1,0:T(8,128)S(1)}, u32[]{:S(2)}, u32[]{:S(2)}) %all-to-all-start.3) | async-done | bytes 2097184 | tf_op jit(solution)/shard_map/all_to_all | solution.py:14
  212.5 0.2 convolution_bitcast_fusion
  212.7 1.8 pad_maximum_fusion
  214.6 0.7 pad_maximum_fusion.1
  215.3 149.4 %all-reduce.2.cloned.1.call-done = f32[2,256,256]{2,1,0:T(8,128)} async-done(((f32[2,256,256]{2,1,0:T(8,128)}), f32[2,256,256]{2,1,0:T(8,128)}) %all-reduce.2.cloned.1.call-update) | async-done | bytes 524304 | tf_op jit(solution)/shard_map/psum | solution.py:77
  364.7 1.9 sub.3
  (22 shorter events, 0.9 us)
Async XLA Ops:
  12.3 3.0 copy-start
  15.3 61.9 %all-to-all-start = ((bf16[16,512,256]{2,1,0:T(8,128)(2,1)}), bf16[16,512,256]{2,1,0:T(8,128)(2,1)}, u32[]{:S(2)}, u32[]{:S(2)}) async-start(bf16[16,512,256]{2,1,0:T(8,128)(2,1)} %stack.12), calls=%async_computation | async-start | bytes 8388608 | tf_op jit(solution)/shard_map/all_to_all | solution.py:46
  79.5 65.7 %all-to-all-start.2 = ((bf16[16,512,256]{2,1,0:T(8,128)(2,1)}), bf16[16,512,256]{2,1,0:T(8,128)(2,1)}, u32[]{:S(2)}, u32[]{:S(2)}) async-start(bf16[16,512,256]{2,1,0:T(8,128)(2,1)} %stack.13), calls=%async_computation.2 | async-start | bytes 8388608 | tf_op jit(solution)/shard_map/all_to_all | solution.py:46
  145.2 31.9 %all-to-all-start.1 = ((f32[8,4,64,256]{3,2,1,0:T(8,128)}), f32[8,4,64,256]{3,2,1,0:T(8,128)}, u32[]{:S(2)}, u32[]{:S(2)}) async-start(f32[8,4,64,256]{3,2,1,0:T(8,128)} %copy.17), calls=%async_computation.1 | async-start | bytes 4194304 | tf_op jit(solution)/shard_map/all_to_all | solution.py:14
  177.1 35.2 %all-to-all-start.3 = ((f32[8,4,64,256]{3,2,1,0:T(8,128)}), f32[8,4,64,256]{3,2,1,0:T(8,128)S(1)}, u32[]{:S(2)}, u32[]{:S(2)}) async-start(f32[8,4,64,256]{3,2,1,0:T(8,128)} %copy.19), calls=%async_computation.3 | async-start | bytes 4194304 | tf_op jit(solution)/shard_map/all_to_all | solution.py:14
  185.3 179.3 %all-reduce.2.cloned.1.call-start = ((), (), s32[]{:S(2)}) async-start(), calls=%async_computation.4 | async-start | bytes 1048576 | tf_op jit(solution)/shard_map/psum | solution.py:77
  212.5 152.2 %copy-start.1 = (f32[2,256,256]{2,1,0:T(8,128)S(1)}, f32[2,256,256]{2,1,0:T(8,128)}, u32[]{:S(2)}) copy-start(f32[2,256,256]{2,1,0:T(8,128)} %param.11) | copy-start | bytes 1572868
Sparse Core Ops, SparseCore 0:
  214.7 149.9 all-reduce.1
